TPU v7x, 128 devices: a whole 4x4x4 slice. The times are simulated.
128 devices in a mesh: sub: 16 (over y, z), grp: 8 (over x, core).
Axes of the slice: x: 4, y: 4, z: 4, core: 2. Of those that a mesh axis runs over, the one named last changes fastest.
Arguments:
- interior_res: bfloat16 [1024, 32, 256], P(('sub', 'grp')), may hold values from -6 to 6
- interface_res: bfloat16 [1024, 32, 512], P(('sub', 'grp')), may hold values from -6 to 6
- interior_inv: bfloat16 [1024, 256, 256], P(('sub', 'grp')), may hold values from -0.375 to 0.375
- coupling: bfloat16 [1024, 512, 256], P(('sub', 'grp')), may hold values from -0.375 to 0.375
- schur_inv: bfloat16 [1024, 512, 512], P(('sub', 'grp')), may hold values from -0.25 to 0.25
- coarse_inv: bfloat16 [512, 128, 128], P('grp'), may hold values from -0.5 to 0.5
- coarse_part: int32 [524288, 1], P(('sub', 'grp')), may hold values from 0 to 127; in each aligned block of 4096 rows (0 to 4095, 4096 to 8191, ...) at most 64 rows name the same one
- coarse_slot: int32 [524288], P(('sub', 'grp')), may hold values from 0 to 511
- live_count: int32 [1024], P(('sub', 'grp')), may hold values from 128 to 512
Outputs:
- interior_update: bfloat16 [1024, 32, 256], P(('sub', 'grp'))
- interface_update: bfloat16 [1024, 32, 512], P(('sub', 'grp'))
Inputs may be any that keep to these rules, and one draw needn't show every extreme that they name: `coarse_part`: in each device's aligned block of 4096 rows no section is named by more than 64 rows, a bound that some block reaches.
All inputs are finite; a program needn't handle non-finite values.
Results may differ from a plain program's by a relative error of at most 0.0076.
Values may be sent and summed in bfloat16 or wider, within the bound.
No kernel may reach another device: no remote copies, remote signals or barrier semaphores. Data moves between devices by JAX's collectives and lax.ppermute only.
A program may use at most 64 MiB of HBM per device.

v0:
```python
import math
import jax
import jax.numpy as jnp
from jax import lax
from jax.sharding import PartitionSpec as P


def coarse_apply(right_side, inverse_blocks):
    vec_count = right_side.shape[0]
    block_size = inverse_blocks.shape[1]
    reshaped = right_side.reshape(vec_count, -1, block_size)
    solved = jnp.einsum(
        "kbj,bij->kbi", reshaped, inverse_blocks, preferred_element_type=jnp.float32
    )
    return solved.reshape(vec_count, -1).astype(jnp.bfloat16)


def spread_cols(values, target, total):
    width = math.gcd(total, 512)

    def spread_one_block(number):
        columns = number * width + lax.iota(jnp.int32, width)
        table = (target[:, None] == columns[None, :]).astype(jnp.bfloat16)
        return jnp.dot(values, table, preferred_element_type=jnp.float32)

    blocks = lax.map(spread_one_block, jnp.arange(total // width, dtype=jnp.int32))
    return jnp.transpose(blocks, (1, 0, 2)).reshape(values.shape[0], total)


def pick_cols(values, wanted):
    count = wanted.shape[0]
    width = math.gcd(count, 512)
    source = lax.iota(jnp.int32, values.shape[1])

    def pick_one_block(number):
        chosen = lax.dynamic_slice_in_dim(wanted, number * width, width, 0)
        table = (source[:, None] == chosen[None, :]).astype(jnp.bfloat16)
        return jnp.dot(values, table, preferred_element_type=jnp.float32)

    blocks = lax.map(pick_one_block, jnp.arange(count // width, dtype=jnp.int32))
    return jnp.transpose(blocks, (1, 0, 2)).reshape(values.shape[0], count).astype(jnp.bfloat16)


def place_in_section(section_list, sections):
    rows_dev = section_list.shape[0]
    width = math.gcd(rows_dev, 128)
    section_hot = (section_list[:, None] == jnp.arange(sections, dtype=jnp.int32)[None, :]).astype(
        jnp.float32
    )
    hot_blocks = section_hot.reshape(rows_dev // width, width, sections)
    lower = (
        lax.broadcasted_iota(jnp.int32, (width, width), 0)
        >= lax.broadcasted_iota(jnp.int32, (width, width), 1)
    ).astype(jnp.float32)
    within = jnp.einsum("ij,bjs->bis", lower, hot_blocks, precision=lax.Precision.HIGHEST)
    totals = within[:, -1, :]
    before = jnp.cumsum(totals, axis=0) - totals
    counted = (within + before[:, None, :]).reshape(rows_dev, sections)
    return jnp.sum((counted - 1.0) * section_hot, axis=1).astype(jnp.int32)


def with_slots(flattened, slot_values):
    upper = (slot_values // 256).astype(jnp.bfloat16)[None, :]
    lower = (slot_values % 256).astype(jnp.bfloat16)[None, :]
    return jnp.concatenate([flattened, upper, lower], axis=0)


def read_slots(received, vec_count):
    upper = received[vec_count].astype(jnp.int32)
    lower = received[vec_count + 1].astype(jnp.int32)
    return (received[:vec_count], upper * 256 + lower)


def on_device(
    interior_res,
    interface_res,
    interior_inv,
    coupling,
    schur_inv,
    coarse_inv,
    coarse_part,
    coarse_slot,
    live_count,
):
    sub_count, vec_count, interior = interior_res.shape
    boundary = interface_res.shape[2]
    owners = lax.axis_size("grp")
    subgroups = lax.axis_size("sub")
    sections = owners * subgroups
    rows_dev = sub_count * boundary
    capacity = 2 * rows_dev // sections
    piece_size = rows_dev // 8
    per_owner = coarse_inv.shape[0] * coarse_inv.shape[1]
    interior_pre = jnp.einsum(
        "sij,skj->ski", interior_inv, interior_res, preferred_element_type=jnp.float32
    ).astype(jnp.bfloat16)
    condensed = interface_res.astype(jnp.float32) - jnp.einsum(
        "sbi,ski->skb", coupling, interior_pre, preferred_element_type=jnp.float32
    )
    alive_mask = (
        lax.broadcasted_iota(jnp.int32, (sub_count, 1, boundary), 2) < live_count[:, None, None]
    )
    condensed = jnp.where(alive_mask, condensed, 0.0).astype(jnp.bfloat16)
    section_list = coarse_part[:, 0]
    owner_list = section_list % owners
    piece_list = section_list // owners
    position = place_in_section(section_list, sections)
    flattened = jnp.transpose(condensed, (1, 0, 2)).reshape(vec_count, rows_dev)
    destination = owner_list * (subgroups * capacity) + piece_list * capacity + position
    owner_slot = piece_list * piece_size + coarse_slot
    outgoing = spread_cols(
        with_slots(flattened, owner_slot), destination, sections * capacity
    ).astype(jnp.bfloat16)
    received = lax.all_to_all(outgoing, "grp", split_axis=1, concat_axis=1, tiled=True)
    recv_rows, recv_slots = read_slots(received, vec_count)
    partial_sum = spread_cols(recv_rows, recv_slots, per_owner)
    summed = lax.psum(partial_sum, "sub")
    coarse_sol = coarse_apply(summed.astype(jnp.bfloat16), coarse_inv)
    replies = pick_cols(coarse_sol, recv_slots)
    returned = lax.all_to_all(replies, "grp", split_axis=1, concat_axis=1, tiled=True)
    correction = pick_cols(returned, destination)
    correction = jnp.transpose(correction.reshape(vec_count, sub_count, boundary), (1, 0, 2))
    local_term = jnp.einsum(
        "sbc,skc->skb", schur_inv, condensed, preferred_element_type=jnp.float32
    )
    interface_update = jnp.where(
        alive_mask, local_term + correction.astype(jnp.float32), 0.0
    ).astype(jnp.bfloat16)
    extended = interior_res.astype(jnp.float32) - jnp.einsum(
        "sbi,skb->ski", coupling, interface_update, preferred_element_type=jnp.float32
    )
    interior_update = jnp.einsum(
        "sij,skj->ski",
        interior_inv,
        extended.astype(jnp.bfloat16),
        preferred_element_type=jnp.float32,
    ).astype(jnp.bfloat16)
    return (interior_update, interface_update)


def solution(mesh):
    in_specs = (
        P(("sub", "grp"), None, None),
        P(("sub", "grp"), None, None),
        P(("sub", "grp"), None, None),
        P(("sub", "grp"), None, None),
        P(("sub", "grp"), None, None),
        P("grp", None, None),
        P(("sub", "grp"), None),
        P(("sub", "grp")),
        P(("sub", "grp")),
    )
    out_specs = (P(("sub", "grp"), None, None), P(("sub", "grp"), None, None))
    return jax.shard_map(
        on_device, mesh=mesh, in_specs=in_specs, out_specs=out_specs, check_vma=False
    )
```

profile of v0, /device:TPU:1, one launch (start us, length us, event | category | flops | bytes accessed | tf_op | source)
XLA Modules:
  0.0 473.6 jit_solution(12313746118868401771)
XLA Ops:
  10.9 69.0 %while.46 = (s32[]{:T(128)}, bf16[16,34,512]{2,1,0:T(8,128)(2,1)}, s32[4096]{0:T(1024)}, s32[16]{0:T(128)S(1)}, bf16[34,4096]{1,0:T(8,128)(2,1)}, /*index=5*/s32[1]{0:T(128)}) while((s32[]{:T(128)}, bf16[16,34,512]{2,1,0:T(8,128)(2,1)}, s32[4096]{0:T(1024)}, s32[16]{0:T(128)S(1)}, bf16[34,4096]{1,0:T(8,128)(2,1)}, ...), condition=%wide.region_3.4_spmd.clone, body=%wide.region_2.3_spmd.sunk.clone | while | flops 144704000 | bytes 430689 | solution.py:26
  12.2 3.1 fusion.94
  16.5 3.1 fusion.94
  20.8 3.1 fusion.94
  25.1 3.1 fusion.94
  29.4 3.1 fusion.94
  33.7 3.1 fusion.94
  38.0 3.1 fusion.94
  42.3 3.1 fusion.94
  51.0 3.1 fusion.94
  55.3 3.1 fusion.94
  59.6 3.1 fusion.94
  68.2 3.1 fusion.94
  72.5 3.1 fusion.94
  86.2 5.8 %all-to-all-start = ((bf16[34,8,1024]{2,0,1:T(8,128)(2,1)}), bf16[34,8,1024]{2,0,1:T(8,128)(2,1)}, u32[]{:S(2)}, u32[]{:S(2)}) async-start(bf16[34,8,1024]{2,0,1:T(8,128)(2,1)} %copy.27), calls=%async_computation | async-start | bytes 1310720 | tf_op jit(solution)/shard_map/all_to_all | solution.py:114
  92.8 10.0 %all-to-all-done = bf16[34,8,1024]{2,0,1:T(8,128)(2,1)} async-done(((bf16[34,8,1024]{2,0,1:T(8,128)(2,1)}), bf16[34,8,1024]{2,0,1:T(8,128)(2,1)}, u32[]{:S(2)}, u32[]{:S(2)}) %all-to-all-start) | async-done | bytes 557088 | tf_op jit(solution)/shard_map/all_to_all | solution.py:114
  106.5 88.7 %while.47 = (s32[]{:T(128)}, f32[16,32,512]{2,1,0:T(8,128)}, s32[8192]{0:T(1024)}, s32[16]{0:T(128)S(1)}, bf16[32,8192]{1,0:T(8,128)(2,1)}, /*index=5*/s32[1]{0:T(128)}) while((s32[]{:T(128)}, f32[16,32,512]{2,1,0:T(8,128)}, s32[8192]{0:T(1024)}, s32[16]{0:T(128)S(1)}, bf16[32,8192]{1,0:T(8,128)(2,1)}, /*index=5*/s32[1]{0:T(128)}) %tuple.96), condition=%wide.region_5.6_spmd.clone, body=%wide.region_4.5_spmd.sunk.clone | while | flops 272630272 | bytes 627297 | solution.py:26
  107.7 4.4 fusion.97
  113.2 4.4 fusion.97
  118.8 4.4 fusion.97
  124.3 4.4 fusion.97
  129.9 4.4 fusion.97
  135.4 4.4 fusion.97
  140.9 4.4 fusion.97
  146.5 4.4 fusion.97
  152.0 4.4 fusion.97
  157.6 4.4 fusion.97
  163.1 4.4 fusion.97
  168.7 4.4 fusion.97
  174.2 4.4 fusion.97
  179.8 4.4 fusion.97
  185.3 4.4 fusion.97
  190.9 4.4 fusion.97
  197.6 76.3 %all-reduce.1 = bf16[32,8192]{1,0:T(8,128)(2,1)} all-reduce(f32[32,8192]{1,0:T(8,128)} %bitcast.120), channel_id=1, replica_groups=mesh['sub'=16,'grp'=8] {'sub'}, use_global_device_ids=true, to_apply=%region_6.7 | all-reduce | flops 262144 | bytes 1572864 | tf_op jit(solution)/shard_map/psum | solution.py:117
  277.0 101.6 %while.48 = (s32[]{:T(128)}, bf16[16,32,512]{2,1,0:T(8,128)(2,1)}, s32[16]{0:T(128)S(1)}, s32[8192]{0:T(1024)}, bf16[32,8192]{1,0:T(8,128)(2,1)}, /*index=5*/s32[1]{0:T(128)}) while((s32[]{:T(128)}, bf16[16,32,512]{2,1,0:T(8,128)(2,1)}, s32[16]{0:T(128)S(1)}, s32[8192]{0:T(1024)}, bf16[32,8192]{1,0:T(8,128)(2,1)}, ...), condition=%wide.region_8.9_spmd.clone.clone, body=%wide.region_7.8_spmd.clone.sunk.clone | while | flops 272629760 | bytes 596611 | solution.py:40
  279.0 4.4 fusion.99
  285.4 4.4 fusion.99
  291.7 4.4 fusion.99
  298.1 4.4 fusion.99
  304.4 4.4 fusion.99
  310.8 4.4 fusion.99
  317.1 4.4 fusion.99
  323.5 4.4 fusion.99
  329.8 4.4 fusion.99
  336.2 4.4 fusion.99
  342.5 4.4 fusion.99
  348.9 4.4 fusion.99
  355.2 4.4 fusion.99
  361.6 4.4 fusion.99
  367.9 4.4 fusion.99
  374.3 4.4 fusion.99
  384.9 19.1 %all-to-all-start.1 = ((bf16[32,8,1024]{2,0,1:T(8,128)(2,1)}), bf16[32,8,1024]{2,0,1:T(8,128)(2,1)}, u32[]{:S(2)}, u32[]{:S(2)}) async-start(bf16[32,8,1024]{2,0,1:T(8,128)(2,1)} %copy.33), calls=%async_computation.1 | async-start | bytes 1048576 | tf_op jit(solution)/shard_map/all_to_all | solution.py:120
  404.0 9.5 %all-to-all-done.1 = bf16[32,8,1024]{2,0,1:T(8,128)(2,1)} async-done(((bf16[32,8,1024]{2,0,1:T(8,128)(2,1)}), bf16[32,8,1024]{2,0,1:T(8,128)(2,1)}, u32[]{:S(2)}, u32[]{:S(2)}) %all-to-all-start.1) | async-done | bytes 524320 | tf_op jit(solution)/shard_map/all_to_all | solution.py:120
  415.3 50.9 %while.49 = (s32[]{:T(128)}, bf16[8,32,512]{2,1,0:T(8,128)(2,1)}, s32[8]{0:T(128)S(1)}, s32[4096]{0:T(1024)}, bf16[32,8192]{1,0:T(8,128)(2,1)}, /*index=5*/s32[1]{0:T(128)}) while((s32[]{:T(128)}, bf16[8,32,512]{2,1,0:T(8,128)(2,1)}, s32[8]{0:T(128)S(1)}, s32[4096]{0:T(1024)}, bf16[32,8192]{1,0:T(8,128)(2,1)}, ...), condition=%wide.region_10.11_spmd.clone.clone, body=%wide.region_9.10_spmd.clone.sunk.clone | while | flops 272629760 | bytes 596611 | solution.py:40
  417.3 4.4 fusion.101
  423.7 4.4 fusion.101
  430.0 4.4 fusion.101
  436.4 4.4 fusion.101
  442.8 4.4 fusion.101
  449.1 4.4 fusion.101
  455.5 4.4 fusion.101
  461.9 4.4 fusion.101
  466.2 4.2 fusion.37
  470.5 3.1 convolution_convert_fusion.1
  (161 shorter events, 94.8 us)
Async XLA Ops:
  0.6 273.3 %copy-start = (bf16[64,128,128]{2,1,0:T(8,128)(2,1)S(1)}, bf16[64,128,128]{2,1,0:T(8,128)(2,1)}, u32[]{:S(2)}) copy-start(bf16[64,128,128]{2,1,0:T(8,128)(2,1)} %param.22) | copy-start | bytes 6291460
  0.6 1.8 copy-start.3
  0.7 3.1 copy-start.5
  0.7 4.4 copy-start.6
  0.7 5.0 %copy-start.1 = (bf16[8,256,256]{2,1,0:T(8,128)(2,1)S(1)}, bf16[8,256,256]{2,1,0:T(8,128)(2,1)}, u32[]{:S(2)}) copy-start(bf16[8,256,256]{2,1,0:T(8,128)(2,1)} %param.19) | copy-start | bytes 3145732
  0.7 5.0 %copy-start.2 = (bf16[8,32,256]{2,1,0:T(8,128)(2,1)S(1)}, bf16[8,32,256]{2,1,0:T(8,128)(2,1)}, u32[]{:S(2)}) copy-start(bf16[8,32,256]{2,1,0:T(8,128)(2,1)} %param.17) | copy-start | bytes 393220
  86.2 16.6 %all-to-all-start = ((bf16[34,8,1024]{2,0,1:T(8,128)(2,1)}), bf16[34,8,1024]{2,0,1:T(8,128)(2,1)}, u32[]{:S(2)}, u32[]{:S(2)}) async-start(bf16[34,8,1024]{2,0,1:T(8,128)(2,1)} %copy.27), calls=%async_computation | async-start | bytes 1310720 | tf_op jit(solution)/shard_map/all_to_all | solution.py:114
  384.9 28.5 %all-to-all-start.1 = ((bf16[32,8,1024]{2,0,1:T(8,128)(2,1)}), bf16[32,8,1024]{2,0,1:T(8,128)(2,1)}, u32[]{:S(2)}, u32[]{:S(2)}) async-start(bf16[32,8,1024]{2,0,1:T(8,128)(2,1)} %copy.33), calls=%async_computation.1 | async-start | bytes 1048576 | tf_op jit(solution)/shard_map/all_to_all | solution.py:120
  415.3 50.9 %copy-start.4 = (pred[8,512]{1,0:T(8,128)(4,1)S(1)}, pred[8,512]{1,0:T(8,128)(4,1)}, u32[]{:S(2)}) copy-start(pred[8,512]{1,0:T(8,128)(4,1)} %iota_compare_fusion.17) | copy-start | bytes 12292
where the time goes:
time: 477 us; the launch traced here: 474 us
  matrix products  238 us (50%)
  blocking collectives  76.3 us (16%)
  local copies, waits for them, and re-layouts  71.9 us (15%)
  loops' own time  35.1 us (7%)
  starting transfers between devices  24.8 us (5%)
  waiting for transfers between devices  19.5 us (4%)
  other arithmetic  7.01 us (1%)
    dot_general x32, matrix products, spread_one_block(): return jnp.dot(values, table, preferred_element_type=jnp.float32)  119 us
    dot_general x24, matrix products, pick_one_block(): return jnp.dot(values, table, preferred_element_type=jnp.float32)  105 us
    psum x1, blocking collectives, on_device(): summed = lax.psum(partial_sum, 'sub')  76.3 us
    dynamic_slice x48, local copies, waits for them, and re-layouts, spread_cols(): lax.map(spread_one_block, jnp.arange(total // width, dtype=jnp.int32))  28 us
    another operation x2, loops' own time, spread_cols(): lax.map(spread_one_block, jnp.arange(total // width, dtype=jnp.int32))  19.7 us
    all_to_all x1, starting transfers between devices, on_device(): lax.all_to_all(replies, 'grp', split_axis=1, concat_axis=1, tiled=True)  19.1 us
    dynamic_slice x24, local copies, waits for them, and re-layouts, pick_one_block(): chosen = lax.dynamic_slice_in_dim(wanted, number * width, width, 0)  18.2 us
    another operation x2, loops' own time, pick_cols(): lax.map(pick_one_block, jnp.arange(count // width, dtype=jnp.int32))  15.4 us
  transfers between devices with their start and end apart: 2, of which 2 were waited for; matrix products, arithmetic and copies ran while one was open for 0% of the time, Pallas kernels for 0%

commit v1 on v0

--- a/solution.py
+++ b/solution.py
@@ -82,6 +82,21 @@
     coarse_slot,
     live_count,
 ):
+
+    def note_run(x0, mesh_name):
+        next_value, latest = (x0, 0)
+        n_lanes = lax.axis_size(mesh_name)
+        while 1 << latest < n_lanes:
+            views = []
+            dev = 0
+            while dev < n_lanes:
+                views.append((dev, dev ^ 1 << latest))
+                dev = dev + 1
+            current_block = lax.ppermute(next_value, mesh_name, views)
+            next_value = next_value + current_block
+            latest = latest + 1
+        return next_value
+
     sub_count, vec_count, interior = interior_res.shape
     boundary = interface_res.shape[2]
     owners = lax.axis_size("grp")
@@ -114,7 +129,7 @@
     received = lax.all_to_all(outgoing, "grp", split_axis=1, concat_axis=1, tiled=True)
     recv_rows, recv_slots = read_slots(received, vec_count)
     partial_sum = spread_cols(recv_rows, recv_slots, per_owner)
-    summed = lax.psum(partial_sum, "sub")
+    summed = note_run(partial_sum, "sub")
     coarse_sol = coarse_apply(summed.astype(jnp.bfloat16), coarse_inv)
     replies = pick_cols(coarse_sol, recv_slots)
     returned = lax.all_to_all(replies, "grp", split_axis=1, concat_axis=1, tiled=True)

time: 477 us -> 486 us (1.019)
  waiting for transfers between devices: 19.5 us -> 105 us
  blocking collectives: 76.3 us -> 0 us
    ppermute x0 -> x4, waiting for transfers between devices: none -> 84.7 us  [note_run(): current_block = lax.ppermute(next_value, mesh_name, views)]
    psum x1 -> x0, blocking collectives: 76.3 us -> none  [on_device(): summed = lax.psum(partial_sum, 'sub')]
    all_to_all x1, starting transfers between devices: 19.1 us -> 8.13 us  [on_device(): lax.all_to_all(replies, 'grp', split_axis=1, concat_axis=1, tiled=True)]
    ppermute x0 -> x4, starting transfers between devices: none -> 9.32 us  [note_run(): current_block = lax.ppermute(next_value, mesh_name, views)]
  transfers between devices with their start and end apart: 2 -> 6, of which waited for: 2 -> 6; matrix products, arithmetic and copies ran while one was open for 0% -> 0% of each run, Pallas kernels for 0% -> 0%
where the time goes in v1:
time: 486 us; the launch traced here: 482 us
  matrix products  239 us (49%)
  waiting for transfers between devices  105 us (22%)
  local copies, waits for them, and re-layouts  70.5 us (15%)
  loops' own time  34.9 us (7%)
  starting transfers between devices  23.2 us (5%)
  other arithmetic  8.32 us (2%)
    dot_general x32, matrix products, spread_one_block(): return jnp.dot(values, table, preferred_element_type=jnp.float32)  119 us
    dot_general x24, matrix products, pick_one_block(): return jnp.dot(values, table, preferred_element_type=jnp.float32)  105 us
    ppermute x4, waiting for transfers between devices, note_run(): current_block = lax.ppermute(next_value, mesh_name, views)  84.7 us
    dynamic_slice x48, local copies, waits for them, and re-layouts, spread_cols(): lax.map(spread_one_block, jnp.arange(total // width, dtype=jnp.int32))  27.6 us
    another operation x2, loops' own time, spread_cols(): lax.map(spread_one_block, jnp.arange(total // width, dtype=jnp.int32))  20.8 us
    dynamic_slice x24, local copies, waits for them, and re-layouts, pick_one_block(): chosen = lax.dynamic_slice_in_dim(wanted, number * width, width, 0)  18.2 us
    another operation x2, loops' own time, pick_cols(): lax.map(pick_one_block, jnp.arange(count // width, dtype=jnp.int32))  14.2 us
    all_to_all x1, waiting for transfers between devices, on_device(): lax.all_to_all(outgoing, 'grp', split_axis=1, concat_axis=1, tiled=True)  10.9 us
  transfers between devices with their start and end apart: 6, of which 6 were waited for; matrix products, arithmetic and copies ran while one was open for 0% of the time, Pallas kernels for 0%

profile of v1, /device:TPU:1, one launch (start us, length us, event | category | flops | bytes accessed | tf_op | source)
XLA Modules:
  0.0 481.8 jit_solution(1503422883917202910)
XLA Ops:
  10.9 69.0 %while.46 = (s32[]{:T(128)}, bf16[16,34,512]{2,1,0:T(8,128)(2,1)}, s32[4096]{0:T(1024)}, s32[16]{0:T(128)S(1)}, bf16[34,4096]{1,0:T(8,128)(2,1)}, /*index=5*/s32[1]{0:T(128)}) while((s32[]{:T(128)}, bf16[16,34,512]{2,1,0:T(8,128)(2,1)}, s32[4096]{0:T(1024)}, s32[16]{0:T(128)S(1)}, bf16[34,4096]{1,0:T(8,128)(2,1)}, ...), condition=%wide.region_3.4_spmd.clone, body=%wide.region_2.3_spmd.sunk.clone | while | flops 144704000 | bytes 430689 | solution.py:26
  12.2 3.1 fusion.96
  20.8 3.1 fusion.96
  29.4 3.1 fusion.96
  42.3 3.1 fusion.96
  46.7 3.1 fusion.96
  51.0 3.1 fusion.96
  63.9 3.1 fusion.96
  72.5 3.1 fusion.96
  76.8 3.1 fusion.96
  86.2 5.8 %all-to-all-start = ((bf16[34,8,1024]{2,0,1:T(8,128)(2,1)}), bf16[34,8,1024]{2,0,1:T(8,128)(2,1)}, u32[]{:S(2)}, u32[]{:S(2)}) async-start(bf16[34,8,1024]{2,0,1:T(8,128)(2,1)} %copy.27), calls=%async_computation | async-start | bytes 1310720 | tf_op jit(solution)/shard_map/all_to_all | solution.py:129
  92.0 10.9 %all-to-all-done = bf16[34,8,1024]{2,0,1:T(8,128)(2,1)} async-done(((bf16[34,8,1024]{2,0,1:T(8,128)(2,1)}), bf16[34,8,1024]{2,0,1:T(8,128)(2,1)}, u32[]{:S(2)}, u32[]{:S(2)}) %all-to-all-start) | async-done | bytes 557088 | tf_op jit(solution)/shard_map/all_to_all | solution.py:129
  106.5 90.2 %while.47 = (s32[]{:T(128)}, f32[16,32,512]{2,1,0:T(8,128)}, s32[8192]{0:T(1024)}, s32[16]{0:T(128)S(1)}, bf16[32,8192]{1,0:T(8,128)(2,1)}, /*index=5*/s32[1]{0:T(128)}) while((s32[]{:T(128)}, f32[16,32,512]{2,1,0:T(8,128)}, s32[8192]{0:T(1024)}, s32[16]{0:T(128)S(1)}, bf16[32,8192]{1,0:T(8,128)(2,1)}, /*index=5*/s32[1]{0:T(128)}) %tuple.96), condition=%wide.region_5.6_spmd.clone, body=%wide.region_4.5_spmd.sunk.clone | while | flops 272630272 | bytes 627297 | solution.py:26
  107.7 4.4 fusion.99
  113.4 4.4 fusion.99
  119.0 4.4 fusion.99
  124.7 4.4 fusion.99
  130.3 4.4 fusion.99
  135.9 4.4 fusion.99
  141.6 4.4 fusion.99
  147.2 4.4 fusion.99
  152.8 4.4 fusion.99
  158.5 4.4 fusion.99
  164.1 4.4 fusion.99
  169.7 4.4 fusion.99
  175.4 4.4 fusion.99
  181.0 4.4 fusion.99
  186.6 4.4 fusion.99
  192.3 4.4 fusion.99
  199.7 22.5 %collective-permute-done = f32[32,8192]{1,0:T(8,128)S(1)} collective-permute-done((f32[32,8192]{1,0:T(8,128)S(1)}, f32[32,8192]{1,0:T(8,128)S(1)}, u32[]{:S(2)}, u32[]{:S(2)}) %collective-permute-start) | collective-permute-done | bytes 1048608 | tf_op jit(solution)/shard_map/ppermute | solution.py:95
  222.3 3.3 collective-permute-start.1
  225.6 21.7 %collective-permute-done.1 = f32[32,8192]{1,0:T(8,128)S(1)} collective-permute-done((f32[32,8192]{1,0:T(8,128)S(1)}, f32[32,8192]{1,0:T(8,128)S(1)}, u32[]{:S(2)}, u32[]{:S(2)}) %collective-permute-start.1) | collective-permute-done | bytes 1048608 | tf_op jit(solution)/shard_map/ppermute | solution.py:95
  248.8 21.0 %collective-permute-done.2 = f32[32,8192]{1,0:T(8,128)S(1)} collective-permute-done((f32[32,8192]{1,0:T(8,128)S(1)}, f32[32,8192]{1,0:T(8,128)S(1)}, u32[]{:S(2)}, u32[]{:S(2)}) %collective-permute-start.2) | collective-permute-done | bytes 1048608 | tf_op jit(solution)/shard_map/ppermute | solution.py:95
  274.7 19.5 %collective-permute-done.3 = f32[32,8192]{1,0:T(8,128)} collective-permute-done((f32[32,8192]{1,0:T(8,128)}, f32[32,8192]{1,0:T(8,128)}, u32[]{:S(2)}, u32[]{:S(2)}) %collective-permute-start.3) | collective-permute-done | bytes 1048608 | tf_op jit(solution)/shard_map/ppermute | solution.py:95
  297.8 99.9 %while.48 = (s32[]{:T(128)}, bf16[16,32,512]{2,1,0:T(8,128)(2,1)}, s32[16]{0:T(128)S(1)}, s32[8192]{0:T(1024)}, bf16[32,8192]{1,0:T(8,128)(2,1)}, /*index=5*/s32[1]{0:T(128)}) while((s32[]{:T(128)}, bf16[16,32,512]{2,1,0:T(8,128)(2,1)}, s32[16]{0:T(128)S(1)}, s32[8192]{0:T(1024)}, bf16[32,8192]{1,0:T(8,128)(2,1)}, ...), condition=%wide.region_7.8_spmd.clone.clone, body=%wide.region_6.7_spmd.clone.sunk.clone | while | flops 272629760 | bytes 596611 | solution.py:40
  299.7 4.4 fusion.101
  305.9 4.4 fusion.101
  312.2 4.4 fusion.101
  318.4 4.4 fusion.101
  324.7 4.4 fusion.101
  330.9 4.4 fusion.101
  337.2 4.4 fusion.101
  343.4 4.4 fusion.101
  349.6 4.4 fusion.101
  355.9 4.4 fusion.101
  362.1 4.4 fusion.101
  368.4 4.4 fusion.101
  374.6 4.4 fusion.101
  380.9 4.4 fusion.101
  387.1 4.4 fusion.101
  393.4 4.4 fusion.101
  404.0 8.1 %all-to-all-start.1 = ((bf16[32,8,1024]{2,0,1:T(8,128)(2,1)}), bf16[32,8,1024]{2,0,1:T(8,128)(2,1)}, u32[]{:S(2)}, u32[]{:S(2)}) async-start(bf16[32,8,1024]{2,0,1:T(8,128)(2,1)} %copy.33), calls=%async_computation.1 | async-start | bytes 1048576 | tf_op jit(solution)/shard_map/all_to_all | solution.py:135
  412.1 9.5 %all-to-all-done.1 = bf16[32,8,1024]{2,0,1:T(8,128)(2,1)} async-done(((bf16[32,8,1024]{2,0,1:T(8,128)(2,1)}), bf16[32,8,1024]{2,0,1:T(8,128)(2,1)}, u32[]{:S(2)}, u32[]{:S(2)}) %all-to-all-start.1) | async-done | bytes 524320 | tf_op jit(solution)/shard_map/all_to_all | solution.py:135
  423.5 50.9 %while.49 = (s32[]{:T(128)}, bf16[8,32,512]{2,1,0:T(8,128)(2,1)}, s32[8]{0:T(128)S(1)}, s32[4096]{0:T(1024)}, bf16[32,8192]{1,0:T(8,128)(2,1)}, /*index=5*/s32[1]{0:T(128)}) while((s32[]{:T(128)}, bf16[8,32,512]{2,1,0:T(8,128)(2,1)}, s32[8]{0:T(128)S(1)}, s32[4096]{0:T(1024)}, bf16[32,8192]{1,0:T(8,128)(2,1)}, ...), condition=%wide.region_9.10_spmd.clone.clone, body=%wide.region_8.9_spmd.clone.sunk.clone | while | flops 272629760 | bytes 596611 | solution.py:40
  425.5 4.4 fusion.103
  431.9 4.4 fusion.103
  438.2 4.4 fusion.103
  444.6 4.4 fusion.103
  451.0 4.4 fusion.103
  457.3 4.4 fusion.103
  463.7 4.4 fusion.103
  470.1 4.4 fusion.103
  474.4 4.2 fusion.37
  478.7 3.1 convolution_convert_fusion.1
  (171 shorter events, 113.4 us)
Async XLA Ops:
  0.6 293.6 %copy-start = (bf16[64,128,128]{2,1,0:T(8,128)(2,1)S(1)}, bf16[64,128,128]{2,1,0:T(8,128)(2,1)}, u32[]{:S(2)}) copy-start(bf16[64,128,128]{2,1,0:T(8,128)(2,1)} %param.22) | copy-start | bytes 6291460
  0.6 1.8 copy-start.3
  0.7 3.1 copy-start.5
  0.7 4.4 copy-start.6
  0.7 5.0 %copy-start.1 = (bf16[8,256,256]{2,1,0:T(8,128)(2,1)S(1)}, bf16[8,256,256]{2,1,0:T(8,128)(2,1)}, u32[]{:S(2)}) copy-start(bf16[8,256,256]{2,1,0:T(8,128)(2,1)} %param.19) | copy-start | bytes 3145732
  0.7 5.0 %copy-start.2 = (bf16[8,32,256]{2,1,0:T(8,128)(2,1)S(1)}, bf16[8,32,256]{2,1,0:T(8,128)(2,1)}, u32[]{:S(2)}) copy-start(bf16[8,32,256]{2,1,0:T(8,128)(2,1)} %param.17) | copy-start | bytes 393220
  86.2 16.6 %all-to-all-start = ((bf16[34,8,1024]{2,0,1:T(8,128)(2,1)}), bf16[34,8,1024]{2,0,1:T(8,128)(2,1)}, u32[]{:S(2)}, u32[]{:S(2)}) async-start(bf16[34,8,1024]{2,0,1:T(8,128)(2,1)} %copy.27), calls=%async_computation | async-start | bytes 1310720 | tf_op jit(solution)/shard_map/all_to_all | solution.py:129
  198.0 24.2 %collective-permute-start = (f32[32,8192]{1,0:T(8,128)S(1)}, f32[32,8192]{1,0:T(8,128)S(1)}, u32[]{:S(2)}, u32[]{:S(2)}) collective-permute-start(f32[32,8192]{1,0:T(8,128)S(1)} %bitcast.118), channel_id=1, source_target_pairs={{0,8},{8,0},{16,24},{24,16},{32,40},{40,32},{48,56},{56,48},{64,72... | collective-permute-start | bytes 3145736 | tf_op jit(solution)/shard_map/ppermute | solution.py:95
  222.3 25.0 %collective-permute-start.1 = (f32[32,8192]{1,0:T(8,128)S(1)}, f32[32,8192]{1,0:T(8,128)S(1)}, u32[]{:S(2)}, u32[]{:S(2)}) collective-permute-start(f32[32,8192]{1,0:T(8,128)S(1)} %add.102), channel_id=1, source_target_pairs={{0,16},{8,24},{16,0},{24,8},{32,48},{40,56},{48,32},{56,40},{64,80... | collective-permute-start | bytes 3145736 | tf_op jit(solution)/shard_map/ppermute | solution.py:95
  247.4 22.4 %collective-permute-start.2 = (f32[32,8192]{1,0:T(8,128)S(1)}, f32[32,8192]{1,0:T(8,128)S(1)}, u32[]{:S(2)}, u32[]{:S(2)}) collective-permute-start(f32[32,8192]{1,0:T(8,128)S(1)} %add.103), channel_id=1, source_target_pairs={{0,32},{8,40},{16,48},{24,56},{32,0},{40,8},{48,16},{56,24},{64,96... | collective-permute-start | bytes 3145736 | tf_op jit(solution)/shard_map/ppermute | solution.py:95
  270.9 23.3 %collective-permute-start.3 = (f32[32,8192]{1,0:T(8,128)}, f32[32,8192]{1,0:T(8,128)}, u32[]{:S(2)}, u32[]{:S(2)}) collective-permute-start(f32[32,8192]{1,0:T(8,128)} %add.104), channel_id=1, source_target_pairs={{0,64},{8,72},{16,80},{24,88},{32,96},{40,104},{48,112},{56,120},{... | collective-permute-start | bytes 3145736 | tf_op jit(solution)/shard_map/ppermute | solution.py:95
  404.0 17.6 %all-to-all-start.1 = ((bf16[32,8,1024]{2,0,1:T(8,128)(2,1)}), bf16[32,8,1024]{2,0,1:T(8,128)(2,1)}, u32[]{:S(2)}, u32[]{:S(2)}) async-start(bf16[32,8,1024]{2,0,1:T(8,128)(2,1)} %copy.33), calls=%async_computation.1 | async-start | bytes 1048576 | tf_op jit(solution)/shard_map/all_to_all | solution.py:135
  423.5 50.9 %copy-start.4 = (pred[8,512]{1,0:T(8,128)(4,1)S(1)}, pred[8,512]{1,0:T(8,128)(4,1)}, u32[]{:S(2)}) copy-start(pred[8,512]{1,0:T(8,128)(4,1)} %iota_compare_fusion.17) | copy-start | bytes 12292
